TPU v7x, 32 devices: a whole 2x2x4 slice. The times are simulated.
32 devices in a mesh: groups: 2 (over y), seq: 16 (over z, x, core).
Axes of the slice: x: 2, y: 2, z: 4, core: 2. Of those that a mesh axis runs over, the one named last changes fastest.
Arguments:
- qkv: bfloat16 [4096, 32, 384], P(('groups', 'seq')), parts along dimension 0
- routes: int32 [4096, 32], P(('groups', 'seq')), parts along dimension 0, may hold values from 0 to 1, as said below
Outputs:
- attended: bfloat16 [4096, 32, 128], P(('groups', 'seq')), parts along dimension 0
There are 2 independent parts, one for each index of `groups`. A program takes and returns all parts, laid end to end along the dimension named above; each array names one. Nothing has to cross between parts.
Inputs may be any that keep to these rules, and one draw needn't show every extreme that they name: Every cluster of every head holds between 512 and 1536 tokens, and in every head some cluster holds exactly 1536. Numbering the pairs (head h, cluster c) as h * 2 + c, the tokens of one device name each aligned group of 4 pairs exactly 256 times. Integer counts, offsets and slot indices derived from routes may cross between devices packed several to a 32-bit word.
All inputs are finite; a program needn't handle non-finite values.
Results may differ from a plain program's by a relative error of at most 0.0047.
Values may be sent and summed in bfloat16 or wider, within the bound.
No kernel may reach another device: no remote copies, remote signals or barrier semaphores. Data moves between devices by JAX's collectives and lax.ppermute only.
A program may use at most 128 MiB of HBM per device.

v0:
```python
import math
import jax
import jax.numpy as jnp
from jax import lax
from jax.sharding import PartitionSpec as P

CLEN = 1024


def entering(part, axis, combine, identity):
    place = lax.axis_index(axis)
    gathered = lax.all_gather(part, axis)
    state = jnp.zeros_like(part) + jnp.asarray(identity, part.dtype)

    def one(turn, state):
        return combine(state, lax.dynamic_index_in_dim(gathered, turn, 0, False))

    return lax.fori_loop(0, place, one, state)


def attend(queries, keys, values, start, scale):
    block_rows = queries.shape[1]
    span = keys.shape[1]
    scores = jnp.einsum("pqd,pkd->pqk", queries, keys, preferred_element_type=jnp.float32) * scale
    rows = start + jnp.arange(block_rows, dtype=jnp.int32)[:, None]
    cols = jnp.arange(span, dtype=jnp.int32)[None, :]
    scores = jnp.where((cols <= rows)[None], scores, -1e30)
    peak = jnp.max(scores, axis=2, keepdims=True)
    expo = jnp.exp(scores - peak)
    weights = (expo / jnp.sum(expo, axis=2, keepdims=True)).astype(jnp.bfloat16)
    return jnp.einsum("pqk,pkd->pqd", weights, values, preferred_element_type=jnp.float32).astype(
        jnp.bfloat16
    )


def local(qkv, routes):
    tok, heads, width = qkv.shape
    head_size = width // 3
    nseq = lax.axis_size("seq")
    clusters = nseq * tok // CLEN
    pairs_dev = heads * tok // CLEN
    capacity = 3 * CLEN // 2
    block_rows = CLEN // 2
    share = CLEN // nseq
    rows_peer = pairs_dev * share
    total_pairs = heads * clusters
    scale = 1.0 / math.sqrt(head_size)
    member = routes[:, :, None] == jnp.arange(clusters, dtype=jnp.int32)[None, None, :]
    member_flat = member.reshape(tok, total_pairs)
    counts = jnp.sum(member_flat.astype(jnp.int32), axis=0)
    earlier = (jnp.arange(tok)[:, None] > jnp.arange(tok)[None, :]).astype(jnp.bfloat16)
    before = jnp.dot(earlier, member_flat.astype(jnp.bfloat16), preferred_element_type=jnp.float32)
    rank = jnp.sum(jnp.where(member, before.reshape(tok, heads, clusters), 0.0), axis=2).astype(
        jnp.int32
    )
    prefix = entering(counts, "seq", lambda first, second: first + second, jnp.zeros_like(counts))

    def lookup(table):
        return jnp.sum(jnp.where(member, table.reshape(heads, clusters)[None], 0), axis=2)

    group_counts = counts.reshape(total_pairs // pairs_dev, pairs_dev)
    within = (jnp.cumsum(group_counts, axis=1) - group_counts).reshape(total_pairs)
    slot = lookup(prefix) + rank
    pair_index = jnp.arange(heads, dtype=jnp.int32)[None, :] * clusters + routes
    owner = pair_index // pairs_dev
    local_pair = pair_index % pairs_dev
    position = (owner * rows_peer + lookup(within) + rank).reshape(tok * heads)
    target = (local_pair * capacity + slot).reshape(tok * heads)
    outgoing = (
        jnp.zeros((tok * heads, width), jnp.bfloat16)
        .at[position]
        .set(qkv.reshape(tok * heads, width))
    )
    labels = jnp.zeros((tok * heads,), jnp.int32).at[position].set(target)
    arrived, places = (
        lax.all_to_all(outgoing, "seq", split_axis=0, concat_axis=0, tiled=True),
        lax.all_to_all(labels, "seq", split_axis=0, concat_axis=0, tiled=True),
    )
    tiles = jnp.zeros((pairs_dev * capacity, width), jnp.bfloat16).at[places].set(arrived)
    tiles = tiles.reshape(pairs_dev, capacity, width)
    pieces = []
    for index in range(3):
        start = index * block_rows
        stop = start + block_rows
        pieces.append(
            attend(
                tiles[:, start:stop, :head_size],
                tiles[:, :stop, head_size : 2 * head_size],
                tiles[:, :stop, 2 * head_size :],
                start,
                scale,
            )
        )
    results = jnp.concatenate(pieces, axis=1)
    flat_results = results.reshape(pairs_dev * capacity, head_size)
    replies = flat_results[places]
    returned = lax.all_to_all(replies, "seq", split_axis=0, concat_axis=0, tiled=True)
    return returned[position].reshape(tok, heads, head_size)


def solution(mesh):
    placed = (P(("groups", "seq"), None, None), P(("groups", "seq"), None))
    return jax.shard_map(
        local,
        mesh=mesh,
        in_specs=placed,
        out_specs=P(("groups", "seq"), None, None),
        check_vma=False,
    )
```

profile of v0, /device:TPU:11, one launch (start us, length us, event | category | flops | bytes accessed | tf_op | source)
XLA Modules:
  0.0 283.6 jit_solution(1487217478119262765)
XLA Ops:
  0.0 0.8 convert_reduce_fusion
  0.8 0.1 copy.13
  0.9 0.1 reshape.224
  1.0 0.1 reshape.177
  1.1 15.5 %all-gather = s32[16,1,64]{2,1,0:T(1,128)S(1)} all-gather(s32[1,1,64]{2,1,0:T(1,128)S(1)} %reshape.224), channel_id=1, replica_groups=mesh['groups'=2,'seq'=16] {'seq'}, dimensions={0}, use_global_device_ids=true | all-gather | bytes 4352 | tf_op jit(solution)/shard_map/all_gather | solution.py:12
  16.6 0.2 while.10
  16.9 0.1 broadcast_in_dim.100
  17.0 0.1 copy.19
  17.0 0.2 reduce_window_sum.13
  17.2 0.1 reduce_window_sum.14
  17.3 0.1 copy.14
  17.4 0.1 eq.32
  17.5 0.7 eq.27.clone
  18.2 0.1 compare_bitcast_fusion
  18.3 0.9 fusion.30
  19.2 0.8 select_reduce_fusion
  20.0 0.8 fusion.47
  20.8 0.1 copy.17
  20.9 0.1 reshape.178
  21.1 0.1 copy.20
  21.1 0.1 reshape.204
  21.2 16.1 %scatter_custom_fusion = s32[4096]{0:T(1024)} fusion(s32[4096]{0:T(1024)S(1)} %bitcast.33, s32[4096]{0:T(1024)S(1)} %reshape.204, s32[]{:T(128)} %constant.29.clone.1), kind=kCustom, calls=%fused_computation.84 | custom fusion | bytes 16388 | tf_op jit(solution)/shard_map/scatter | solution.py:74
  37.3 9.8 %all-to-all-start = ((s32[16,256,1]{1,2,0:T(1,128)}), s32[16,256,1]{1,2,0:T(1,128)S(1)}, u32[]{:S(2)}, u32[]{:S(2)}) async-start(s32[16,256,1]{1,2,0:T(1,128)} %bitcast.6), calls=%async_computation | async-start | bytes 32768 | tf_op jit(solution)/shard_map/all_to_all | solution.py:77
  47.1 20.5 %scatter_custom_fusion.1 = bf16[4096,384]{1,0:T(8,128)(2,1)} fusion(s32[4096]{0:T(1024)S(1)} %bitcast.34, bf16[4096,384]{1,0:T(8,128)(2,1)} %bitcast.40, bf16[]{:T(256)} %constant.27.clone.1), kind=kCustom, calls=%fused_computation.41 | custom fusion | bytes 3146240 | tf_op jit(solution)/shard_map/scatter | solution.py:72
  67.7 0.0 all-to-all-done
  67.7 6.1 %all-to-all-start.1 = ((bf16[16,256,384]{2,1,0:T(8,128)(2,1)}), bf16[16,256,384]{2,1,0:T(8,128)(2,1)S(1)}, u32[]{:S(2)}, u32[]{:S(2)}) async-start(bf16[16,256,384]{2,1,0:T(8,128)(2,1)} %bitcast.10), calls=%async_computation.1 | async-start | bytes 6291456 | tf_op jit(solution)/shard_map/all_to_all | solution.py:76
  73.8 0.1 iota_compare_fusion.2
  73.8 1.2 iota_compare_fusion.1
  75.0 1.4 iota_compare_fusion
  76.4 67.2 %all-to-all-done.1 = bf16[16,256,384]{2,1,0:T(8,128)(2,1)S(1)} async-done(((bf16[16,256,384]{2,1,0:T(8,128)(2,1)}), bf16[16,256,384]{2,1,0:T(8,128)(2,1)S(1)}, u32[]{:S(2)}, u32[]{:S(2)}) %all-to-all-start.1) | async-done | bytes 3145760 | tf_op jit(solution)/shard_map/all_to_all | solution.py:76
  143.6 21.1 %scatter_custom_fusion.2 = bf16[6144,384]{1,0:T(8,128)(2,1)} fusion(s32[4096]{0:T(1024)S(1)} %bitcast.38, bf16[4096,384]{1,0:T(8,128)(2,1)S(1)} %bitcast.31, bf16[]{:T(256)} %constant.27.clone.1), kind=kCustom, calls=%fused_computation.30 | custom fusion | bytes 4718594 | tf_op jit(solution)/shard_map/scatter | solution.py:79
  164.8 8.1 %fusion.21 = f32[4,512,1536]{2,1,0:T(8,128)} fusion(bf16[4,1536,384]{2,1,0:T(8,128)(2,1)} %bitcast.25), kind=kOutput, calls=%fused_computation.38 | convolution fusion | flops 805306368 | bytes 14680064 | tf_op jit(solution)/shard_map/pqd,pkd->pqk/dot_general | solution.py:24
  172.8 0.0 copy-done
  172.8 4.5 %fusion.32 = f32[4,512,1024]{2,1,0:T(8,128)} fusion(bf16[4,1536,384]{2,1,0:T(8,128)(2,1)S(1)} %bitcast.26), kind=kOutput, calls=%fused_computation.49 | convolution fusion | flops 536870912 | bytes 9961472 | tf_op jit(solution)/shard_map/pqd,pkd->pqk/dot_general | solution.py:24
  177.3 2.8 fusion.37
  180.1 0.0 copy-done.2
  180.1 16.0 %fusion.58 = (f32[4,512]{1,0:T(4,128)S(1)}, f32[4,512,1536]{2,1,0:T(8,128)}) fusion(f32[4,512,1536]{2,1,0:T(8,128)} %fusion.21, pred[512,1536]{1,0:T(8,128)(4,1)S(1)} %copy-done.2), kind=kOutput, calls=%fused_computation.95 | output fusion | flops 18875904 | bytes 25960448 | tf_op jit(solution)/shard_map/sub | solution.py:29
  196.1 6.6 %fusion.27 = bf16[4,512,128]{2,1,0:T(8,128)(2,1)S(1)} fusion(bf16[4,1536,384]{2,1,0:T(8,128)(2,1)S(1)} %bitcast.28, f32[4,512,1536]{2,1,0:T(8,128)} %get-tuple-element.42, f32[4,512]{1,0:T(4,128)S(1)} %get-tuple-element.41), kind=kOutput, calls=%fused_computation.45 | convolution fusion | flops 811859968 | bytes 14688256 | tf_op jit(solution)/shard_map/pqk,pkd->pqd/dot_general | solution.py:31
  202.6 13.0 %fusion.59 = (f32[4,512]{1,0:T(4,128)S(1)}, f32[4,512,1024]{2,1,0:T(8,128)}) fusion(f32[4,512,1024]{2,1,0:T(8,128)} %fusion.32, pred[512,1024]{1,0:T(8,128)(4,1)S(1)} %copy-done.3), kind=kOutput, calls=%fused_computation.96 | output fusion | flops 12583935 | bytes 17309696 | tf_op jit(solution)/shard_map/sub | solution.py:29
  215.6 4.9 %fusion.25 = bf16[4,512,128]{2,1,0:T(8,128)(2,1)S(1)} fusion(f32[4,512,1024]{2,1,0:T(8,128)} %get-tuple-element.44, f32[4,512]{1,0:T(4,128)S(1)} %get-tuple-element.43, bf16[4,1536,384]{2,1,0:T(8,128)(2,1)S(1)} %bitcast.29), kind=kOutput, calls=%fused_computation.43 | convolution fusion | flops 541327360 | bytes 9969664 | tf_op jit(solution)/shard_map/pqk,pkd->pqd/dot_general | solution.py:31
  220.5 0.0 copy-done.1
  220.5 2.1 fusion.60
  222.7 1.0 fusion.26
  223.6 0.1 pad_maximum_fusion
  223.7 15.0 %gather_fusion = bf16[4096,128]{1,0:T(8,128)(2,1)} fusion(bf16[6144,128]{1,0:T(8,128)(2,1)S(1)} %bitcast.24, s32[4096]{0:T(1024)S(1)} %broadcast_clamp_fusion.1), kind=kCustom, calls=%fused_computation | custom fusion | bytes 2113536 | tf_op jit(solution)/shard_map/gather | solution.py:96
  238.8 4.9 %all-to-all-start.2 = ((bf16[16,256,128]{2,1,0:T(8,128)(2,1)}), bf16[16,256,128]{2,1,0:T(8,128)(2,1)S(1)}, u32[]{:S(2)}, u32[]{:S(2)}) async-start(bf16[16,256,128]{2,1,0:T(8,128)(2,1)} %bitcast.14), calls=%async_computation.2 | async-start | bytes 2097152 | tf_op jit(solution)/shard_map/all_to_all | solution.py:97
  243.7 24.9 %all-to-all-done.2 = bf16[16,256,128]{2,1,0:T(8,128)(2,1)S(1)} async-done(((bf16[16,256,128]{2,1,0:T(8,128)(2,1)}), bf16[16,256,128]{2,1,0:T(8,128)(2,1)S(1)}, u32[]{:S(2)}, u32[]{:S(2)}) %all-to-all-start.2) | async-done | bytes 1048608 | tf_op jit(solution)/shard_map/all_to_all | solution.py:97
  268.5 15.0 %gather_fusion.1 = bf16[4096,128]{1,0:T(8,128)(2,1)} fusion(bf16[4096,128]{1,0:T(8,128)(2,1)S(1)} %bitcast.23, s32[4096]{0:T(1024)S(1)} %broadcast_clamp_fusion), kind=kCustom, calls=%fused_computation.1 | custom fusion | bytes 2113536 | tf_op jit(solution)/shard_map/gather | solution.py:98
  (23 shorter events, 0.2 us)
Async XLA Ops:
  37.3 30.3 %all-to-all-start = ((s32[16,256,1]{1,2,0:T(1,128)}), s32[16,256,1]{1,2,0:T(1,128)S(1)}, u32[]{:S(2)}, u32[]{:S(2)}) async-start(s32[16,256,1]{1,2,0:T(1,128)} %bitcast.6), calls=%async_computation | async-start | bytes 32768 | tf_op jit(solution)/shard_map/all_to_all | solution.py:77
  67.7 76.0 %all-to-all-start.1 = ((bf16[16,256,384]{2,1,0:T(8,128)(2,1)}), bf16[16,256,384]{2,1,0:T(8,128)(2,1)S(1)}, u32[]{:S(2)}, u32[]{:S(2)}) async-start(bf16[16,256,384]{2,1,0:T(8,128)(2,1)} %bitcast.10), calls=%async_computation.1 | async-start | bytes 6291456 | tf_op jit(solution)/shard_map/all_to_all | solution.py:76
  164.7 8.1 %copy-start = (bf16[6144,384]{1,0:T(8,128)(2,1)S(1)}, bf16[6144,384]{1,0:T(8,128)(2,1)}, u32[]{:S(2)}) copy-start(bf16[6144,384]{1,0:T(8,128)(2,1)} %scatter_custom_fusion.2) | copy-start | bytes 14155780
  177.3 2.8 copy-start.2
  196.1 6.6 %copy-start.3 = (pred[512,1024]{1,0:T(8,128)(4,1)S(1)}, pred[512,1024]{1,0:T(8,128)(4,1)}, u32[]{:S(2)}) copy-start(pred[512,1024]{1,0:T(8,128)(4,1)} %iota_compare_fusion.1) | copy-start | bytes 1572868
  215.6 4.9 %copy-start.1 = (f32[4,512,512]{1,2,0:T(8,128)S(1)}, f32[4,512,512]{1,2,0:T(8,128)}, u32[]{:S(2)}) copy-start(f32[4,512,512]{1,2,0:T(8,128)} %fusion.37) | copy-start | bytes 12582916
  238.8 29.8 %all-to-all-start.2 = ((bf16[16,256,128]{2,1,0:T(8,128)(2,1)}), bf16[16,256,128]{2,1,0:T(8,128)(2,1)S(1)}, u32[]{:S(2)}, u32[]{:S(2)}) async-start(bf16[16,256,128]{2,1,0:T(8,128)(2,1)} %bitcast.14), calls=%async_computation.2 | async-start | bytes 2097152 | tf_op jit(solution)/shard_map/all_to_all | solution.py:97
where the time goes:
time: 284 us
  waiting for transfers between devices  92.1 us (32%)
  local copies, waits for them, and re-layouts  89.7 us (32%)
  other arithmetic  36.7 us (13%)
  matrix products  28.6 us (10%)
  starting transfers between devices  20.8 us (7%)
  blocking collectives  15.5 us (5%)
    all_to_all x1, waiting for transfers between devices, local(): lax.all_to_all(outgoing, 'seq', split_axis=0, concat_axis=0, tiled=True)  67.2 us
    sub x3, other arithmetic, attend(): expo = jnp.exp(scores - peak)  31.1 us
    all_to_all x1, waiting for transfers between devices, local(): lax.all_to_all(replies, 'seq', split_axis=0, concat_axis=0, tiled=True)  24.9 us
    scatter x1, local copies, waits for them, and re-layouts, local(): jnp.zeros((pairs_dev * capacity, width), jnp.bfloat16).at[places]  21.1 us
    scatter x1, local copies, waits for them, and re-layouts, local(): outgoing = jnp.zeros((tok * heads, width), jnp.bfloat16).at[position].set...  20.5 us
    scatter x1, local copies, waits for them, and re-layouts, local(): labels = jnp.zeros((tok * heads,), jnp.int32).at[position].set(target)  16.1 us
    all_gather x1, blocking collectives, entering(): gathered = lax.all_gather(part, axis)  15.5 us
    dot_general x3, matrix products, attend(): jnp.einsum('pqd,pkd->pqk', queries, keys, preferred_element_type=jnp.floa...  15.3 us
  transfers between devices with their start and end apart: 3, of which 2 were waited for; matrix products, arithmetic and copies ran while one was open for 8% of the time, Pallas kernels for 0%

commit v1 on v0

--- a/solution.py
+++ b/solution.py
@@ -5,6 +5,17 @@
 from jax.sharding import PartitionSpec as P
 
 CLEN = 1024
+
+
+def in_blocks(x, dim, peers):
+    before, after = (x.shape[:dim], x.shape[dim + 1 :])
+    return jnp.moveaxis(x.reshape(*before, peers, -1, *after), dim, 0)
+
+
+def laid_out(pieces, dim):
+    shape = list(pieces.shape[1:])
+    shape[dim] *= pieces.shape[0]
+    return jnp.moveaxis(pieces, 0, dim).reshape(shape)
 
 
 def entering(part, axis, combine, identity):
@@ -94,7 +105,15 @@
     results = jnp.concatenate(pieces, axis=1)
     flat_results = results.reshape(pairs_dev * capacity, head_size)
     replies = flat_results[places]
-    returned = lax.all_to_all(replies, "seq", split_axis=0, concat_axis=0, tiled=True)
+    size, mine = (lax.axis_size("seq"), lax.axis_index("seq"))
+    parts = in_blocks(replies, 0, size)
+    result = parts
+    for step in range(1, size):
+        target_2, source = ((mine + step) % size, (mine - step) % size)
+        sent = lax.dynamic_index_in_dim(parts, target_2, 0)
+        received = lax.ppermute(sent, "seq", [(i, (i + step) % size) for i in range(size)])
+        result = lax.dynamic_update_slice_in_dim(result, received, source, axis=0)
+    returned = laid_out(result, 0)
     return returned[position].reshape(tok, heads, head_size)
 
 

time: 284 us -> 287 us (1.011)
  starting transfers between devices: 20.8 us -> 37.7 us
  waiting for transfers between devices: 92.1 us -> 79.8 us
    all_to_all x1 -> x0, waiting for transfers between devices: 24.9 us -> none  [local(): lax.all_to_all(replies, 'seq', split_axis=0, concat_axis=0, tiled=True)]
    ppermute x0 -> x15, starting transfers between devices: none -> 21.8 us  [local(): lax.ppermute(sent, 'seq', [(i, (i + step) % size) for i in range(size)])]
    ppermute x0 -> x15, waiting for transfers between devices: none -> 10.8 us  [local(): lax.ppermute(sent, 'seq', [(i, (i + step) % size) for i in range(size)])]
    all_to_all x1 -> x0, starting transfers between devices: 4.9 us -> none  [local(): lax.all_to_all(replies, 'seq', split_axis=0, concat_axis=0, tiled=True)]
    gather x1, local copies, waits for them, and re-layouts: 15 us -> 12.1 us  [local(): replies = flat_results[places]]
  transfers between devices with their start and end apart: 3 -> 17, of which waited for: 2 -> 8; matrix products, arithmetic and copies ran while one was open for 8% -> 8% of each run, Pallas kernels for 0% -> 0%
where the time goes in v1:
time: 287 us; the launch traced here: 285 us
  local copies, waits for them, and re-layouts  87.5 us (30%)
  waiting for transfers between devices  79.8 us (28%)
  starting transfers between devices  37.7 us (13%)
  other arithmetic  34.9 us (12%)
  matrix products  28.5 us (10%)
  blocking collectives  15.5 us (5%)
    all_to_all x1, waiting for transfers between devices, local(): lax.all_to_all(outgoing, 'seq', split_axis=0, concat_axis=0, tiled=True)  69 us
    sub x3, other arithmetic, attend(): expo = jnp.exp(scores - peak)  31 us
    ppermute x15, starting transfers between devices, local(): lax.ppermute(sent, 'seq', [(i, (i + step) % size) for i in range(size)])  21.8 us
    scatter x1, local copies, waits for them, and re-layouts, local(): jnp.zeros((pairs_dev * capacity, width), jnp.bfloat16).at[places]  21.3 us
    scatter x1, local copies, waits for them, and re-layouts, local(): outgoing = jnp.zeros((tok * heads, width), jnp.bfloat16).at[position].set...  20.6 us
    scatter x1, local copies, waits for them, and re-layouts, local(): labels = jnp.zeros((tok * heads,), jnp.int32).at[position].set(target)  16.1 us
    all_gather x1, blocking collectives, entering(): gathered = lax.all_gather(part, axis)  15.5 us
    dot_general x3, matrix products, attend(): jnp.einsum('pqd,pkd->pqk', queries, keys, preferred_element_type=jnp.floa...  15.3 us
  transfers between devices with their start and end apart: 17, of which 8 were waited for; matrix products, arithmetic and copies ran while one was open for 8% of the time, Pallas kernels for 0%

profile of v1, /device:TPU:11, one launch (start us, length us, event | category | flops | bytes accessed | tf_op | source)
XLA Modules:
  0.0 284.6 jit_solution(5605388151883515149)
XLA Ops:
  0.0 0.8 convert_reduce_fusion
  0.9 0.1 reshape.230
  1.1 15.5 %all-gather = s32[16,1,64]{2,1,0:T(1,128)S(1)} all-gather(s32[1,1,64]{2,1,0:T(1,128)S(1)} %reshape.230), channel_id=1, replica_groups=mesh['groups'=2,'seq'=16] {'seq'}, dimensions={0}, use_global_device_ids=true | all-gather | bytes 4352 | tf_op jit(solution)/shard_map/all_gather | solution.py:23
  16.6 0.2 while.10
  17.0 0.2 reduce_window_sum.13
  17.4 0.1 eq.63
  17.5 0.7 eq.58.clone
  18.3 0.9 fusion.30
  19.2 0.8 select_reduce_fusion
  20.0 0.8 fusion.47
  20.8 0.1 copy.17
  20.9 0.1 reshape.182
  21.2 16.1 %scatter_custom_fusion = s32[4096]{0:T(1024)} fusion(s32[4096]{0:T(1024)S(1)} %bitcast.35, s32[4096]{0:T(1024)S(1)} %reshape.210, s32[]{:T(128)} %constant.242.clone.1), kind=kCustom, calls=%fused_computation.84 | custom fusion | bytes 16388 | tf_op jit(solution)/shard_map/scatter | solution.py:85
  37.3 9.8 %all-to-all-start = ((s32[16,256,1]{1,2,0:T(1,128)}), s32[16,256,1]{1,2,0:T(1,128)S(1)}, u32[]{:S(2)}, u32[]{:S(2)}) async-start(s32[16,256,1]{1,2,0:T(1,128)} %bitcast.6), calls=%async_computation | async-start | bytes 32768 | tf_op jit(solution)/shard_map/all_to_all | solution.py:88
  47.1 20.6 %scatter_custom_fusion.1 = bf16[4096,384]{1,0:T(8,128)(2,1)} fusion(s32[4096]{0:T(1024)S(1)} %bitcast.36, bf16[4096,384]{1,0:T(8,128)(2,1)} %bitcast.42, bf16[]{:T(256)} %constant.241.clone.1), kind=kCustom, calls=%fused_computation.41 | custom fusion | bytes 3146240 | tf_op jit(solution)/shard_map/scatter | solution.py:83
  67.7 6.1 %all-to-all-start.1 = ((bf16[16,256,384]{2,1,0:T(8,128)(2,1)}), bf16[16,256,384]{2,1,0:T(8,128)(2,1)}, u32[]{:S(2)}, u32[]{:S(2)}) async-start(bf16[16,256,384]{2,1,0:T(8,128)(2,1)} %bitcast.33), calls=%async_computation.1 | async-start | bytes 6291456 | tf_op jit(solution)/shard_map/all_to_all | solution.py:87
  73.9 0.4 iota_compare_fusion.1
  74.2 0.5 iota_compare_fusion
  74.8 69.0 %all-to-all-done.1 = bf16[16,256,384]{2,1,0:T(8,128)(2,1)} async-done(((bf16[16,256,384]{2,1,0:T(8,128)(2,1)}), bf16[16,256,384]{2,1,0:T(8,128)(2,1)}, u32[]{:S(2)}, u32[]{:S(2)}) %all-to-all-start.1) | async-done | bytes 3145760 | tf_op jit(solution)/shard_map/all_to_all | solution.py:87
  143.8 21.3 %scatter_custom_fusion.2 = bf16[6144,384]{1,0:T(8,128)(2,1)} fusion(s32[4096]{0:T(1024)S(1)} %bitcast.40, bf16[4096,384]{1,0:T(8,128)(2,1)} %bitcast.11, bf16[]{:T(256)} %constant.241.clone.1), kind=kCustom, calls=%fused_computation.30 | custom fusion | bytes 4719104 | tf_op jit(solution)/shard_map/scatter | solution.py:90
  165.1 8.1 %fusion.21 = f32[4,512,1536]{2,1,0:T(8,128)} fusion(bf16[4,1536,384]{2,1,0:T(8,128)(2,1)} %bitcast.27), kind=kOutput, calls=%fused_computation.38 | convolution fusion | flops 805306368 | bytes 14680064 | tf_op jit(solution)/shard_map/pqd,pkd->pqk/dot_general | solution.py:35
  173.2 4.5 %fusion.32 = f32[4,512,1024]{2,1,0:T(8,128)} fusion(bf16[4,1536,384]{2,1,0:T(8,128)(2,1)S(1)} %bitcast.28), kind=kOutput, calls=%fused_computation.49 | convolution fusion | flops 536870912 | bytes 9961472 | tf_op jit(solution)/shard_map/pqd,pkd->pqk/dot_general | solution.py:35
  177.7 2.8 fusion.37
  180.4 16.0 %fusion.58 = (f32[4,512]{1,0:T(4,128)S(1)}, f32[4,512,1536]{2,1,0:T(8,128)}) fusion(f32[4,512,1536]{2,1,0:T(8,128)} %fusion.21, pred[512,1536]{1,0:T(8,128)(4,1)S(1)} %iota_compare_fusion), kind=kOutput, calls=%fused_computation.125 | output fusion | flops 18875904 | bytes 25960448 | tf_op jit(solution)/shard_map/sub | solution.py:40
  196.4 6.5 %fusion.27 = bf16[4,512,128]{2,1,0:T(8,128)(2,1)S(1)} fusion(bf16[4,1536,384]{2,1,0:T(8,128)(2,1)S(1)} %bitcast.30, f32[4,512,1536]{2,1,0:T(8,128)} %get-tuple-element.57, f32[4,512]{1,0:T(4,128)S(1)} %get-tuple-element.56), kind=kOutput, calls=%fused_computation.45 | convolution fusion | flops 811859968 | bytes 14688256 | tf_op jit(solution)/shard_map/pqk,pkd->pqd/dot_general | solution.py:42
  202.9 12.9 %fusion.59 = (f32[4,512]{1,0:T(4,128)S(1)}, f32[4,512,1024]{2,1,0:T(8,128)}) fusion(f32[4,512,1024]{2,1,0:T(8,128)} %fusion.32, pred[512,1024]{1,0:T(8,128)(4,1)S(1)} %iota_compare_fusion.1), kind=kOutput, calls=%fused_computation.126 | output fusion | flops 12583935 | bytes 17309696 | tf_op jit(solution)/shard_map/sub | solution.py:40
  215.8 4.9 %fusion.25 = bf16[4,512,128]{2,1,0:T(8,128)(2,1)S(1)} fusion(f32[4,512,1024]{2,1,0:T(8,128)} %get-tuple-element.59, f32[4,512]{1,0:T(4,128)S(1)} %get-tuple-element.58, bf16[4,1536,384]{2,1,0:T(8,128)(2,1)S(1)} %bitcast.31), kind=kOutput, calls=%fused_computation.43 | convolution fusion | flops 541327360 | bytes 9969664 | tf_op jit(solution)/shard_map/pqk,pkd->pqd/dot_general | solution.py:42
  220.8 2.1 fusion.60
  222.9 1.0 fusion.26
  223.9 0.1 pad_maximum_fusion
  224.0 12.1 %gather_fusion = bf16[4096,128]{1,0:T(8,128)(2,1)S(1)} fusion(bf16[6144,128]{1,0:T(8,128)(2,1)S(1)} %bitcast.26, s32[4096]{0:T(1024)S(1)} %broadcast_clamp_fusion.1), kind=kCustom, calls=%fused_computation | custom fusion | bytes 2113536 | tf_op jit(solution)/shard_map/gather | solution.py:107
  236.1 1.9 collective-permute-start
  238.1 1.3 collective-permute-done
  239.4 0.2 constant_dynamic-slice_fusion
  240.0 0.7 collective-permute-start.2
  240.7 4.1 %collective-permute-start.3 = (bf16[1,256,128]{2,1,0:T(8,128)(2,1)S(1)}, bf16[1,256,128]{2,1,0:T(8,128)(2,1)S(1)}, u32[]{:S(2)}, u32[]{:S(2)}) collective-permute-start(bf16[1,256,128]{2,1,0:T(8,128)(2,1)S(1)} %get-tuple-element.50), channel_id=1, source_target_pairs={{0,4},{1,5},{2,6},{3,7},{4,8},{5,9},{6,10},{7,11},{8,12},{9,13},{1... | collective-permute-start | bytes 196616 | tf_op jit(solution)/shard_map/ppermute | solution.py:114
  244.8 0.1 collective-permute-start.4
  244.9 3.1 %collective-permute-start.5 = (bf16[1,256,128]{2,1,0:T(8,128)(2,1)S(1)}, bf16[1,256,128]{2,1,0:T(8,128)(2,1)S(1)}, u32[]{:S(2)}, u32[]{:S(2)}) collective-permute-start(bf16[1,256,128]{2,1,0:T(8,128)(2,1)S(1)} %get-tuple-element.48), channel_id=1, source_target_pairs={{0,6},{1,7},{2,8},{3,9},{4,10},{5,11},{6,12},{7,13},{8,14},{9,15},... | collective-permute-start | bytes 196616 | tf_op jit(solution)/shard_map/ppermute | solution.py:114
  248.0 1.8 collective-permute-start.7
  249.9 1.6 collective-permute-start.8
  251.5 3.5 %collective-permute-done.4 = bf16[1,256,128]{2,1,0:T(8,128)(2,1)S(1)} collective-permute-done((bf16[1,256,128]{2,1,0:T(8,128)(2,1)S(1)}, bf16[1,256,128]{2,1,0:T(8,128)(2,1)S(1)}, u32[]{:S(2)}, u32[]{:S(2)}) %collective-permute-start.4) | collective-permute-done | bytes 65568 | tf_op jit(solution)/shard_map/ppermute | solution.py:114
  255.0 1.4 collective-permute-done.5
  256.4 4.5 %collective-permute-start.10 = (bf16[1,256,128]{2,1,0:T(8,128)(2,1)S(1)}, bf16[1,256,128]{2,1,0:T(8,128)(2,1)S(1)}, u32[]{:S(2)}, u32[]{:S(2)}) collective-permute-start(bf16[1,256,128]{2,1,0:T(8,128)(2,1)S(1)} %get-tuple-element.43), channel_id=1, source_target_pairs={{0,11},{1,12},{2,13},{3,14},{4,15},{5,0},{6,1},{7,2},{8,3},{9,4},{... | collective-permute-start | bytes 196616 | tf_op jit(solution)/shard_map/ppermute | solution.py:114
  261.2 3.6 %collective-permute-start.13 = (bf16[1,256,128]{2,1,0:T(8,128)(2,1)S(1)}, bf16[1,256,128]{2,1,0:T(8,128)(2,1)S(1)}, u32[]{:S(2)}, u32[]{:S(2)}) collective-permute-start(bf16[1,256,128]{2,1,0:T(8,128)(2,1)S(1)} %get-tuple-element.40), channel_id=1, source_target_pairs={{0,14},{1,15},{2,0},{3,1},{4,2},{5,3},{6,4},{7,5},{8,6},{9,7},{10,... | collective-permute-start | bytes 196616 | tf_op jit(solution)/shard_map/ppermute | solution.py:114
  265.0 1.1 collective-permute-done.11
  266.2 2.7 collective-permute-done.13
  268.9 0.7 collective-permute-done.14
  269.6 15.0 %gather_fusion.1 = bf16[4096,128]{1,0:T(8,128)(2,1)} fusion(bf16[4096,128]{1,0:T(8,128)(2,1)S(1)} %bitcast.25, s32[4096]{0:T(1024)S(1)} %broadcast_clamp_fusion), kind=kCustom, calls=%fused_computation.1 | custom fusion | bytes 2113536 | tf_op jit(solution)/shard_map/gather | solution.py:117
  (63 shorter events, 1.6 us)
Async XLA Ops:
  37.3 30.4 %all-to-all-start = ((s32[16,256,1]{1,2,0:T(1,128)}), s32[16,256,1]{1,2,0:T(1,128)S(1)}, u32[]{:S(2)}, u32[]{:S(2)}) async-start(s32[16,256,1]{1,2,0:T(1,128)} %bitcast.6), calls=%async_computation | async-start | bytes 32768 | tf_op jit(solution)/shard_map/all_to_all | solution.py:88
  67.7 76.1 %all-to-all-start.1 = ((bf16[16,256,384]{2,1,0:T(8,128)(2,1)}), bf16[16,256,384]{2,1,0:T(8,128)(2,1)}, u32[]{:S(2)}, u32[]{:S(2)}) async-start(bf16[16,256,384]{2,1,0:T(8,128)(2,1)} %bitcast.33), calls=%async_computation.1 | async-start | bytes 6291456 | tf_op jit(solution)/shard_map/all_to_all | solution.py:87
  165.1 8.1 %copy-start = (bf16[6144,384]{1,0:T(8,128)(2,1)S(1)}, bf16[6144,384]{1,0:T(8,128)(2,1)}, u32[]{:S(2)}) copy-start(bf16[6144,384]{1,0:T(8,128)(2,1)} %scatter_custom_fusion.2) | copy-start | bytes 14155780
  215.8 4.9 %copy-start.1 = (f32[4,512,512]{1,2,0:T(8,128)S(1)}, f32[4,512,512]{1,2,0:T(8,128)}, u32[]{:S(2)}) copy-start(f32[4,512,512]{1,2,0:T(8,128)} %fusion.37) | copy-start | bytes 12582916
  236.1 3.3 %collective-permute-start = (bf16[1,256,128]{2,1,0:T(8,128)(2,1)S(1)}, bf16[1,256,128]{2,1,0:T(8,128)(2,1)S(1)}, u32[]{:S(2)}, u32[]{:S(2)}) collective-permute-start(bf16[1,256,128]{2,1,0:T(8,128)(2,1)S(1)} %constant_dynamic-slice_fusion.14), channel_id=1, source_target_pairs={{0,1},{1,2},{2,3},{3,4},{4,5},{5,6},{6,7},{7,8},{8,9},{9,10},{10,1... | collective-permute-start | bytes 196616 | tf_op jit(solution)/shard_map/ppermute | solution.py:114
  239.6 8.4 %collective-permute-start.1 = (bf16[1,256,128]{2,1,0:T(8,128)(2,1)S(1)}, bf16[1,256,128]{2,1,0:T(8,128)(2,1)S(1)}, u32[]{:S(2)}, u32[]{:S(2)}) collective-permute-start(bf16[1,256,128]{2,1,0:T(8,128)(2,1)S(1)} %get-tuple-element.52), channel_id=1, source_target_pairs={{0,2},{1,3},{2,4},{3,5},{4,6},{5,7},{6,8},{7,9},{8,10},{9,11},{10,... | collective-permute-start | bytes 196616 | tf_op jit(solution)/shard_map/ppermute | solution.py:114
  240.0 8.0 %collective-permute-start.2 = (bf16[1,256,128]{2,1,0:T(8,128)(2,1)S(1)}, bf16[1,256,128]{2,1,0:T(8,128)(2,1)S(1)}, u32[]{:S(2)}, u32[]{:S(2)}) collective-permute-start(bf16[1,256,128]{2,1,0:T(8,128)(2,1)S(1)} %get-tuple-element.51), channel_id=1, source_target_pairs={{0,3},{1,4},{2,5},{3,6},{4,7},{5,8},{6,9},{7,10},{8,11},{9,12},{10... | collective-permute-start | bytes 196616 | tf_op jit(solution)/shard_map/ppermute | solution.py:114
  240.7 9.2 %collective-permute-start.3 = (bf16[1,256,128]{2,1,0:T(8,128)(2,1)S(1)}, bf16[1,256,128]{2,1,0:T(8,128)(2,1)S(1)}, u32[]{:S(2)}, u32[]{:S(2)}) collective-permute-start(bf16[1,256,128]{2,1,0:T(8,128)(2,1)S(1)} %get-tuple-element.50), channel_id=1, source_target_pairs={{0,4},{1,5},{2,6},{3,7},{4,8},{5,9},{6,10},{7,11},{8,12},{9,13},{1... | collective-permute-start | bytes 196616 | tf_op jit(solution)/shard_map/ppermute | solution.py:114
  244.8 10.2 %collective-permute-start.4 = (bf16[1,256,128]{2,1,0:T(8,128)(2,1)S(1)}, bf16[1,256,128]{2,1,0:T(8,128)(2,1)S(1)}, u32[]{:S(2)}, u32[]{:S(2)}) collective-permute-start(bf16[1,256,128]{2,1,0:T(8,128)(2,1)S(1)} %get-tuple-element.49), channel_id=1, source_target_pairs={{0,5},{1,6},{2,7},{3,8},{4,9},{5,10},{6,11},{7,12},{8,13},{9,14},{... | collective-permute-start | bytes 196616 | tf_op jit(solution)/shard_map/ppermute | solution.py:114
  244.9 11.5 %collective-permute-start.5 = (bf16[1,256,128]{2,1,0:T(8,128)(2,1)S(1)}, bf16[1,256,128]{2,1,0:T(8,128)(2,1)S(1)}, u32[]{:S(2)}, u32[]{:S(2)}) collective-permute-start(bf16[1,256,128]{2,1,0:T(8,128)(2,1)S(1)} %get-tuple-element.48), channel_id=1, source_target_pairs={{0,6},{1,7},{2,8},{3,9},{4,10},{5,11},{6,12},{7,13},{8,14},{9,15},... | collective-permute-start | bytes 196616 | tf_op jit(solution)/shard_map/ppermute | solution.py:114
  248.0 13.0 %collective-permute-start.6 = (bf16[1,256,128]{2,1,0:T(8,128)(2,1)S(1)}, bf16[1,256,128]{2,1,0:T(8,128)(2,1)S(1)}, u32[]{:S(2)}, u32[]{:S(2)}) collective-permute-start(bf16[1,256,128]{2,1,0:T(8,128)(2,1)S(1)} %get-tuple-element.47), channel_id=1, source_target_pairs={{0,7},{1,8},{2,9},{3,10},{4,11},{5,12},{6,13},{7,14},{8,15},{9,0},... | collective-permute-start | bytes 196616 | tf_op jit(solution)/shard_map/ppermute | solution.py:114
  248.0 13.1 %collective-permute-start.7 = (bf16[1,256,128]{2,1,0:T(8,128)(2,1)S(1)}, bf16[1,256,128]{2,1,0:T(8,128)(2,1)S(1)}, u32[]{:S(2)}, u32[]{:S(2)}) collective-permute-start(bf16[1,256,128]{2,1,0:T(8,128)(2,1)S(1)} %get-tuple-element.46), channel_id=1, source_target_pairs={{0,8},{1,9},{2,10},{3,11},{4,12},{5,13},{6,14},{7,15},{8,0},{9,1},... | collective-permute-start | bytes 196616 | tf_op jit(solution)/shard_map/ppermute | solution.py:114
  249.9 11.3 %collective-permute-start.8 = (bf16[1,256,128]{2,1,0:T(8,128)(2,1)S(1)}, bf16[1,256,128]{2,1,0:T(8,128)(2,1)S(1)}, u32[]{:S(2)}, u32[]{:S(2)}) collective-permute-start(bf16[1,256,128]{2,1,0:T(8,128)(2,1)S(1)} %get-tuple-element.45), channel_id=1, source_target_pairs={{0,9},{1,10},{2,11},{3,12},{4,13},{5,14},{6,15},{7,0},{8,1},{9,2},... | collective-permute-start | bytes 196616 | tf_op jit(solution)/shard_map/ppermute | solution.py:114
  255.0 9.8 %collective-permute-start.9 = (bf16[1,256,128]{2,1,0:T(8,128)(2,1)S(1)}, bf16[1,256,128]{2,1,0:T(8,128)(2,1)S(1)}, u32[]{:S(2)}, u32[]{:S(2)}) collective-permute-start(bf16[1,256,128]{2,1,0:T(8,128)(2,1)S(1)} %get-tuple-element.44), channel_id=1, source_target_pairs={{0,10},{1,11},{2,12},{3,13},{4,14},{5,15},{6,0},{7,1},{8,2},{9,3},... | collective-permute-start | bytes 196616 | tf_op jit(solution)/shard_map/ppermute | solution.py:114
  256.4 8.5 %collective-permute-start.10 = (bf16[1,256,128]{2,1,0:T(8,128)(2,1)S(1)}, bf16[1,256,128]{2,1,0:T(8,128)(2,1)S(1)}, u32[]{:S(2)}, u32[]{:S(2)}) collective-permute-start(bf16[1,256,128]{2,1,0:T(8,128)(2,1)S(1)} %get-tuple-element.43), channel_id=1, source_target_pairs={{0,11},{1,12},{2,13},{3,14},{4,15},{5,0},{6,1},{7,2},{8,3},{9,4},{... | collective-permute-start | bytes 196616 | tf_op jit(solution)/shard_map/ppermute | solution.py:114
  261.0 5.1 %collective-permute-start.11 = (bf16[1,256,128]{2,1,0:T(8,128)(2,1)S(1)}, bf16[1,256,128]{2,1,0:T(8,128)(2,1)S(1)}, u32[]{:S(2)}, u32[]{:S(2)}) collective-permute-start(bf16[1,256,128]{2,1,0:T(8,128)(2,1)S(1)} %get-tuple-element.42), channel_id=1, source_target_pairs={{0,12},{1,13},{2,14},{3,15},{4,0},{5,1},{6,2},{7,3},{8,4},{9,5},{1... | collective-permute-start | bytes 196616 | tf_op jit(solution)/shard_map/ppermute | solution.py:114
  261.1 5.0 %collective-permute-start.12 = (bf16[1,256,128]{2,1,0:T(8,128)(2,1)S(1)}, bf16[1,256,128]{2,1,0:T(8,128)(2,1)S(1)}, u32[]{:S(2)}, u32[]{:S(2)}) collective-permute-start(bf16[1,256,128]{2,1,0:T(8,128)(2,1)S(1)} %get-tuple-element.41), channel_id=1, source_target_pairs={{0,13},{1,14},{2,15},{3,0},{4,1},{5,2},{6,3},{7,4},{8,5},{9,6},{10... | collective-permute-start | bytes 196616 | tf_op jit(solution)/shard_map/ppermute | solution.py:114
  261.2 7.7 %collective-permute-start.13 = (bf16[1,256,128]{2,1,0:T(8,128)(2,1)S(1)}, bf16[1,256,128]{2,1,0:T(8,128)(2,1)S(1)}, u32[]{:S(2)}, u32[]{:S(2)}) collective-permute-start(bf16[1,256,128]{2,1,0:T(8,128)(2,1)S(1)} %get-tuple-element.40), channel_id=1, source_target_pairs={{0,14},{1,15},{2,0},{3,1},{4,2},{5,3},{6,4},{7,5},{8,6},{9,7},{10,... | collective-permute-start | bytes 196616 | tf_op jit(solution)/shard_map/ppermute | solution.py:114
  264.9 4.7 %collective-permute-start.14 = (bf16[1,256,128]{2,1,0:T(8,128)(2,1)S(1)}, bf16[1,256,128]{2,1,0:T(8,128)(2,1)S(1)}, u32[]{:S(2)}, u32[]{:S(2)}) collective-permute-start(bf16[1,256,128]{2,1,0:T(8,128)(2,1)S(1)} %get-tuple-element.39), channel_id=1, source_target_pairs={{0,15},{1,0},{2,1},{3,2},{4,3},{5,4},{6,5},{7,6},{8,7},{9,8},{10,9... | collective-permute-start | bytes 196616 | tf_op jit(solution)/shard_map/ppermute | solution.py:114
